TPU v7x, 512 devices: a whole 4x4x16 slice. The times are simulated.
512 devices in a mesh: section: 4 (over x), trial: 128 (over z, y, core).
Axes of the slice: x: 4, y: 4, z: 16, core: 2. Of those that a mesh axis runs over, the one named last changes fastest.
Arguments:
- spike_rates: bfloat16 [512, 256, 256], P(None, 'trial'), may hold values from -6 to 6
- first_preactivation: bfloat16 [1024, 256, 256], P('section', 'trial'), may hold values from -6 to 6
- second_preactivation: bfloat16 [1024, 256, 256], P('section', 'trial'), may hold values from -6 to 6
- output_gradient: bfloat16 [1024, 256, 256], P('section', 'trial'), may hold values from -0.29882812 to 0.29882812
- first_kernel: bfloat16 [3, 1024, 1024], P(None, None, 'section'), may hold values from -0.109375 to 0.109375
- second_kernel: bfloat16 [3, 1024, 1024], P(None, None, 'section'), may hold values from -0.109375 to 0.109375
- session_of: int32 [256], P('trial'), may hold values from 0 to 127, never falling along the last dimension, each value on 1 to 6 neighbouring positions
Outputs:
- readin_grad: bfloat16 [128, 512, 1024], P(None, 'trial', 'section')
Inputs may be any that keep to these rules, and one draw needn't show every extreme that they name: `session_of`: the trials of a session are consecutive; every session has 1 to 6 trials, and one has exactly 6.
All inputs are finite; a program needn't handle non-finite values.
Results may differ from a plain program's by a relative error of at most 0.017.
Values may be sent and summed in bfloat16 or wider, within the bound.
No kernel may reach another device: no remote copies, remote signals or barrier semaphores. Data moves between devices by JAX's collectives and lax.ppermute only.
A program may use at most 64 MiB of HBM per device.

v0:
```python
import math
import jax
import jax.numpy as jnp
from jax import lax
from jax.sharding import PartitionSpec as P

FIRST_DILATION = 32
SECOND_DILATION = 64
MOST = 6


def gelu_slope(preact):
    values = preact.astype(jnp.float32)
    normal_cdf = 0.5 * (1.0 + lax.erf(values * (1.0 / math.sqrt(2.0))))
    density = jnp.exp(-0.5 * values * values) * (1.0 / math.sqrt(2.0 * math.pi))
    return normal_cdf + values * density


def shift_ahead(values, offset):
    padding = [(0, 0)] * (values.ndim - 1) + [(0, offset)]
    return jnp.pad(values[..., offset:], padding)


def tap_sum(weights, flow_grad, spacing):
    running = None
    for kernel_tap in range(3):
        term_tap = lax.dot_general(
            weights[kernel_tap],
            flow_grad,
            (((1,), (0,)), ((), ())),
            preferred_element_type=jnp.float32,
        )
        if kernel_tap > 0:
            term_tap = shift_ahead(term_tap, kernel_tap * spacing)
        running = term_tap if running is None else running + term_tap
    return running


def layer_backprop(upstream, preact, turned, spacing):
    flow_grad = (upstream.astype(jnp.float32) * gelu_slope(preact)).astype(jnp.bfloat16)
    back_sum = tap_sum(turned, lax.all_gather(flow_grad, "section", axis=0, tiled=True), spacing)
    return (upstream.astype(jnp.float32) + back_sum).astype(jnp.bfloat16)


def body(
    spike_rates,
    first_preactivation,
    second_preactivation,
    output_gradient,
    first_kernel,
    second_kernel,
    session_of,
):
    first_flipped_kernel, second_flipped_kernel = (
        lax.all_to_all(first_kernel, "section", split_axis=1, concat_axis=2, tiled=True),
        lax.all_to_all(second_kernel, "section", split_axis=1, concat_axis=2, tiled=True),
    )
    upstream_gradient = layer_backprop(
        output_gradient, second_preactivation, second_flipped_kernel, SECOND_DILATION
    )
    input_gradient = layer_backprop(
        upstream_gradient, first_preactivation, first_flipped_kernel, FIRST_DILATION
    )
    trial_shards = lax.axis_size("trial")
    neurons, trials, steps_count = spike_rates.shape
    neuron_blocks = spike_rates.reshape(trial_shards, neurons // trial_shards, trials, steps_count)
    partials = jnp.einsum(
        "jbil,cil->jibc", neuron_blocks, input_gradient, preferred_element_type=jnp.float32
    )
    arrived = lax.all_to_all(
        partials.astype(jnp.bfloat16), "trial", split_axis=0, concat_axis=0, tiled=True
    ).astype(partials.dtype)
    every_id = lax.all_gather(session_of, "trial", axis=0, tiled=True)
    total_trials = every_id.shape[0]
    flat_parts = arrived.reshape(total_trials, -1)
    session_list = jnp.arange(trial_shards, dtype=jnp.int32)
    first_trial = jnp.sum((every_id[None, :] < session_list[:, None]).astype(jnp.int32), axis=1)

    def add_offset(offset, running):
        position = first_trial + offset
        clipped = jnp.minimum(position, total_trials - 1)
        rows_here = jnp.take(flat_parts, clipped, axis=0)
        valid = (position < total_trials) & (jnp.take(every_id, clipped, axis=0) == session_list)
        return running + jnp.where(valid[:, None], rows_here, 0.0)

    start_sums = jnp.zeros((trial_shards, flat_parts.shape[1]), jnp.float32)
    summed = lax.fori_loop(0, MOST, add_offset, start_sums)
    return summed.reshape(trial_shards, neurons // trial_shards, input_gradient.shape[0]).astype(
        jnp.bfloat16
    )


def solution(mesh):
    in_specs = (
        P(None, "trial", None),
        P("section", "trial", None),
        P("section", "trial", None),
        P("section", "trial", None),
        P(None, None, "section"),
        P(None, None, "section"),
        P("trial"),
    )
    out_specs = P(None, "trial", "section")
    return jax.shard_map(body, mesh=mesh, in_specs=in_specs, out_specs=out_specs, check_vma=False)
```

profile of v0, /device:TPU:8, one launch (start us, length us, event | category | flops | bytes accessed | tf_op | source)
XLA Modules:
  0.0 186.1 jit_solution(364001516441620479)
XLA Ops:
  6.5 1.2 copy.50
  9.9 2.7 %copy.52 = bf16[3,1024,256]{2,0,1:T(4,128)(2,1)} copy(bf16[3,1024,256]{2,1,0:T(8,128)(2,1)S(1)} %copy-done.3) | data formatting | bytes 3145728 | tf_op args[5]
  12.6 4.4 %all-to-all-start = ((bf16[3,1024,256]{2,0,1:T(4,128)(2,1)}), bf16[3,1024,256]{2,0,1:T(4,128)(2,1)S(1)}, u32[]{:S(2)}, u32[]{:S(2)}) async-start(bf16[3,1024,256]{2,0,1:T(4,128)(2,1)} %copy.52), calls=%async_computation | async-start | bytes 4194304 | tf_op jit(solution)/shard_map/all_to_all | solution.py:56
  17.2 29.0 %all-to-all-done = bf16[3,1024,256]{2,0,1:T(4,128)(2,1)S(1)} async-done(((bf16[3,1024,256]{2,0,1:T(4,128)(2,1)}), bf16[3,1024,256]{2,0,1:T(4,128)(2,1)S(1)}, u32[]{:S(2)}, u32[]{:S(2)}) %all-to-all-start) | async-done | bytes 1572896 | tf_op jit(solution)/shard_map/all_to_all | solution.py:56
  46.2 1.5 copy.79
  49.4 6.2 %all-gather.3.cloned.1.call-done = bf16[1024,2,256]{0,2,1:T(8,128)(2,1)} async-done(((bf16[256,2,256]{0,2,1:T(8,128)(2,1)}), bf16[1024,2,256]{0,2,1:T(8,128)(2,1)}) %all-gather.3.cloned.1.call-update) | async-done | bytes 1048592 | tf_op jit(solution)/shard_map/all_gather | solution.py:41
  55.6 1.8 convolution_bitcast_fusion.4
  57.9 1.5 fusion.31
  59.4 1.4 copy.55
  60.8 31.6 %all_to_all.35 = bf16[3,1024,256]{2,0,1:T(4,128)(2,1)S(1)} all-to-all(bf16[3,1024,256]{2,0,1:T(4,128)(2,1)S(1)} %copy.55), channel_id=1, replica_groups=mesh['section'=4,'trial'=128] {'section'}, dimensions={1} | all-to-all | bytes 3145728 | tf_op jit(solution)/shard_map/all_to_all | solution.py:55
  93.3 7.2 %all-gather.5.cloned.1.call-done = bf16[1024,2,256]{0,2,1:T(8,128)(2,1)} async-done(((bf16[256,2,256]{0,2,1:T(8,128)(2,1)}), bf16[1024,2,256]{0,2,1:T(8,128)(2,1)}) %all-gather.5.cloned.1.call-update) | async-done | bytes 1048592 | tf_op jit(solution)/shard_map/all_gather | solution.py:41
  100.5 1.8 convolution_bitcast_fusion.1
  102.8 2.0 %fusion.3 = bf16[128,2,4,256]{0,3,2,1:T(8,128)(2,1)S(1)} fusion(f32[256,2,256]{0,2,1:T(8,128)} %get-tuple-element.154, bf16[1024,2,256]{0,2,1:T(8,128)(2,1)S(1)} %copy-done.1, bf16[256,1024,1]{0,1,2:T(8,128)(2,1)S(1)} %bitcast.90, bf16[128,4,2,256]{3,2,1,0:T(2,128)(2,1)S(1)} %bitcast.84, f32[256,2,192]{0,2,1:T(8,128)S(1)} %slice.59, ...), kind=kOutput, calls=%fused_computation.13 | convolution fusion | flops 403439616 | bytes 3997696 | tf_op jit(solution)/shard_map/jbil,cil->jibc/dot_general | solution.py:67
  104.8 1.2 copy.65
  106.0 19.0 %all-to-all-start.2 = ((bf16[128,2,4,256]{3,2,1,0:T(4,128)(2,1)}), bf16[128,2,4,256]{3,2,1,0:T(4,128)(2,1)S(1)}, u32[]{:S(2)}, u32[]{:S(2)}) async-start(bf16[128,2,4,256]{3,2,1,0:T(4,128)(2,1)} %copy.65), calls=%async_computation.2 | async-start | bytes 1048576 | tf_op jit(solution)/shard_map/all_to_all | solution.py:70
  125.0 1.2 dynamic-slice
  127.1 37.2 %all-reduce.4 = s32[256]{0:T(256)S(1)} all-reduce(s32[256]{0:T(256)S(1)} %dynamic-update-slice), channel_id=1, replica_groups=mesh['section'=4,'trial'=128] {'trial'}, use_global_device_ids=true, to_apply=%add.4 | all-reduce | flops 256 | bytes 2048
  164.5 13.8 %while.14 = (s32[]{:T(128)}, f32[128,1024]{1,0:T(8,128)S(1)}, s32[128]{0:T(128)S(1)}, s32[256]{0:T(256)S(1)}, f32[256,1024]{1,0:T(8,128)S(1)}, /*index=5*/s32[]{:T(128)}, s32[]{:T(128)}) while((s32[]{:T(128)}, f32[128,1024]{1,0:T(8,128)S(1)}, s32[128]{0:T(128)S(1)}, s32[256]{0:T(256)S(1)}, f32[256,1024]{1,0:T(8,128)S(1)}, ...), condition=%wide.region_2.3_spmd.clone, body=%wide.region_1.2_spmd.clone.sunk | while | flops 527491 | bytes 2630751 | solution.py:87
  164.6 1.3 gather_fusion.1
  166.9 1.3 gather_fusion.1
  169.2 1.3 gather_fusion.1
  171.5 1.3 gather_fusion.1
  173.7 1.3 gather_fusion.1
  176.0 1.3 gather_fusion.1
  (74 shorter events, 13.1 us)
Async XLA Ops:
  6.5 96.3 %copy-start = (bf16[512,2,256]{2,1,0:T(2,128)(2,1)S(1)}, bf16[512,2,256]{2,1,0:T(2,128)(2,1)}, u32[]{:S(2)}) copy-start(bf16[512,2,256]{2,1,0:T(2,128)(2,1)} %param.9) | copy-start | bytes 1572868
  6.5 3.4 %copy-start.3 = (bf16[3,1024,256]{2,1,0:T(8,128)(2,1)S(1)}, bf16[3,1024,256]{2,1,0:T(8,128)(2,1)}, u32[]{:S(2)}) copy-start(bf16[3,1024,256]{2,1,0:T(8,128)(2,1)} %param.14) | copy-start | bytes 4718596
  6.5 49.0 %all-gather.3.cloned.1.call-start = ((), (), s32[]{:S(2)}) async-start(), calls=%async_computation.3 | async-start | bytes 1310720 | tf_op jit(solution)/shard_map/all_gather | solution.py:41
  12.6 4.4 %copy-start.5 = (bf16[256,2,256]{2,1,0:T(2,128)(2,1)S(1)}, bf16[256,2,256]{2,1,0:T(2,128)(2,1)}, u32[]{:S(2)}) copy-start(bf16[256,2,256]{2,1,0:T(2,128)(2,1)} %param.10) | copy-start | bytes 786436
  12.6 33.6 %all-to-all-start = ((bf16[3,1024,256]{2,0,1:T(4,128)(2,1)}), bf16[3,1024,256]{2,0,1:T(4,128)(2,1)S(1)}, u32[]{:S(2)}, u32[]{:S(2)}) async-start(bf16[3,1024,256]{2,0,1:T(4,128)(2,1)} %copy.52), calls=%async_computation | async-start | bytes 4194304 | tf_op jit(solution)/shard_map/all_to_all | solution.py:56
  17.0 83.5 %all-gather.5.cloned.1.call-start = ((), (), s32[]{:S(2)}) async-start(), calls=%async_computation.4 | async-start | bytes 1310720 | tf_op jit(solution)/shard_map/all_gather | solution.py:41
  55.6 1.8 copy-start.2
  57.9 1.5 copy-start.4
  100.5 1.8 copy-start.1
  104.8 22.1 %copy-start.6 = (s32[2]{0:T(128)S(1)}, s32[2]{0:T(128)}, u32[]{:S(2)}) copy-start(s32[2]{0:T(128)} %param.15) | copy-start | bytes 28
  106.0 58.4 %all-to-all-start.2 = ((bf16[128,2,4,256]{3,2,1,0:T(4,128)(2,1)}), bf16[128,2,4,256]{3,2,1,0:T(4,128)(2,1)S(1)}, u32[]{:S(2)}, u32[]{:S(2)}) async-start(bf16[128,2,4,256]{3,2,1,0:T(4,128)(2,1)} %copy.65), calls=%async_computation.2 | async-start | bytes 1048576 | tf_op jit(solution)/shard_map/all_to_all | solution.py:70
Sparse Core Ops, SparseCore 0:
  10.0 45.5 all-gather.2
  59.5 40.9 all-gather.4
where the time goes:
time: 187 us; the launch traced here: 186 us
  blocking collectives  68.8 us (37%)
  waiting for transfers between devices  42.5 us (23%)
  local copies, waits for them, and re-layouts  26.8 us (14%)
  starting transfers between devices  23.4 us (13%)
  between operations  14.2 us (8%)
  matrix products  7.88 us (4%)
  other arithmetic  2.14 us (1%)
    unnamed x1, blocking collectives  37.2 us
    all_to_all x1, blocking collectives, body(): lax.all_to_all(first_kernel, 'section', split_axis=1, concat_axis=2, tile...  31.6 us
    all_to_all x1, waiting for transfers between devices, body(): lax.all_to_all(second_kernel, 'section', split_axis=1, concat_axis=2, til...  29 us
    all_to_all x1, starting transfers between devices, body(): lax.all_to_all(partials.astype(jnp.bfloat16), 'trial', split_axis=0, conc...  19 us
    all_gather x2, waiting for transfers between devices, layer_backprop(): lax.all_gather(flow_grad, 'section', axis=0, tiled=True)  13.4 us
    unnamed x23, local copies, waits for them, and re-layouts  8.19 us
    gather x6, local copies, waits for them, and re-layouts, add_offset(): jnp.take(every_id, clipped, axis=0) == session_list  7.59 us
    dot_general x5, matrix products, tap_sum(): lax.dot_general(weights[kernel_tap], flow_grad, (((1,), (0,)), ((), ())),...  5.91 us
  transfers between devices with their start and end apart: 4, of which 3 were waited for; matrix products, arithmetic and copies ran while one was open for 5% of the time, Pallas kernels for 0%

commit v1 on v0

--- a/solution.py
+++ b/solution.py
@@ -53,7 +53,15 @@
 ):
     first_flipped_kernel, second_flipped_kernel = (
         lax.all_to_all(first_kernel, "section", split_axis=1, concat_axis=2, tiled=True),
-        lax.all_to_all(second_kernel, "section", split_axis=1, concat_axis=2, tiled=True),
+        jnp.concatenate(
+            lax.all_to_all(
+                jnp.stack(jnp.split(second_kernel, lax.axis_size("section"), axis=1)),
+                "section",
+                0,
+                0,
+            ),
+            axis=2,
+        ),
     )
     upstream_gradient = layer_backprop(
         output_gradient, second_preactivation, second_flipped_kernel, SECOND_DILATION

time: 187 us -> 177 us (0.947)
  waiting for transfers between devices: 42.5 us -> 8.75 us
  blocking collectives: 68.8 us -> 97.4 us
  starting transfers between devices: 23.4 us -> 19.6 us
  local copies, waits for them, and re-layouts: 26.8 us -> 23.8 us
    all_to_all x1 -> x0, waiting for transfers between devices: 29 us -> none  [body(): lax.all_to_all(second_kernel, 'section', split_axis=1, concat_axis=2, til...]
    all_to_all x0 -> x1, blocking collectives: none -> 24.8 us  [body(): lax.all_to_all(jnp.stack(jnp.split(second_kernel, lax.axis_size('section'...]
    unnamed x23 -> x19, local copies, waits for them, and re-layouts: 8.19 us -> 3.08 us
    all_gather x2, waiting for transfers between devices: 13.4 us -> 8.72 us  [layer_backprop(): lax.all_gather(flow_grad, 'section', axis=0, tiled=True)]
    all_to_all x1 -> x0, starting transfers between devices: 4.42 us -> none  [body(): lax.all_to_all(second_kernel, 'section', split_axis=1, concat_axis=2, til...]
    all_to_all x1, blocking collectives: 31.6 us -> 35.6 us  [body(): lax.all_to_all(first_kernel, 'section', split_axis=1, concat_axis=2, tile...]
  transfers between devices with their start and end apart: 4 -> 3, of which waited for: 3 -> 2; matrix products, arithmetic and copies ran while one was open for 5% -> 5% of each run, Pallas kernels for 0% -> 0%
where the time goes in v1:
time: 177 us; the launch traced here: 176 us
  blocking collectives  97.4 us (55%)
  local copies, waits for them, and re-layouts  23.8 us (13%)
  starting transfers between devices  19.6 us (11%)
  between operations  14.3 us (8%)
  waiting for transfers between devices  8.75 us (5%)
  matrix products  8.48 us (5%)
  other arithmetic  3.43 us (2%)
    unnamed x1, blocking collectives  37 us
    all_to_all x1, blocking collectives, body(): lax.all_to_all(first_kernel, 'section', split_axis=1, concat_axis=2, tile...  35.6 us
    all_to_all x1, blocking collectives, body(): lax.all_to_all(jnp.stack(jnp.split(second_kernel, lax.axis_size('section'...  24.8 us
    all_to_all x1, starting transfers between devices, body(): lax.all_to_all(partials.astype(jnp.bfloat16), 'trial', split_axis=0, conc...  19.6 us
    all_gather x2, waiting for transfers between devices, layer_backprop(): lax.all_gather(flow_grad, 'section', axis=0, tiled=True)  8.72 us
    gather x6, local copies, waits for them, and re-layouts, add_offset(): jnp.take(every_id, clipped, axis=0) == session_list  7.59 us
    dot_general x5, matrix products, tap_sum(): lax.dot_general(weights[kernel_tap], flow_grad, (((1,), (0,)), ((), ())),...  5.88 us
    gather x6, local copies, waits for them, and re-layouts, add_offset(): rows_here = jnp.take(flat_parts, clipped, axis=0)  4.8 us
  transfers between devices with their start and end apart: 3, of which 2 were waited for; matrix products, arithmetic and copies ran while one was open for 5% of the time, Pallas kernels for 0%

profile of v1, /device:TPU:8, one launch (start us, length us, event | category | flops | bytes accessed | tf_op | source)
XLA Modules:
  0.0 176.2 jit_solution(1094010181891371230)
XLA Ops:
  6.5 2.0 %fusion.15 = bf16[256,2,256]{2,0,1:T(8,128)(2,1)} fusion(bf16[256,2,256]{2,1,0:T(2,128)(2,1)} %param.11, bf16[256,2,256]{2,1,0:T(2,128)(2,1)} %param.12), kind=kLoop, calls=%fused_computation.38 | loop fusion | flops 1572864 | bytes 786432 | tf_op jit(solution)/shard_map/convert_element_type | solution.py:40
  8.7 1.5 slice_bitcast_fusion.3
  10.3 24.8 %all_to_all.25 = bf16[4,3,256,256]{3,2,1,0:T(8,128)(2,1)S(1)} all-to-all(bf16[4,3,256,256]{3,2,1,0:T(8,128)(2,1)S(1)} %pad_maximum_fusion), channel_id=1, replica_groups=mesh['section'=4,'trial'=128] {'section'}, dimensions={0} | all-to-all | bytes 3145728 | tf_op jit(solution)/shard_map/all_to_all | solution.py:57
  37.7 8.0 %all-gather.3.cloned.1.call-done = bf16[1024,2,256]{2,0,1:T(8,128)(2,1)} async-done(((bf16[256,2,256]{2,0,1:T(8,128)(2,1)}), bf16[1024,2,256]{2,0,1:T(8,128)(2,1)}) %all-gather.3.cloned.1.call-update) | async-done | bytes 1048592 | tf_op jit(solution)/shard_map/all_gather | solution.py:41
  45.7 1.9 %fusion.13 = f32[256,2,192]{2,0,1:T(8,128)S(1)} fusion(bf16[256,1024,1]{1,0,2:T(8,128)(2,1)S(1)} %reshape.110, bf16[1024,2,256]{2,0,1:T(8,128)(2,1)} %all-gather.3.cloned.1.call-done), kind=kOutput, calls=%fused_computation.27 | convolution fusion | flops 201326592 | bytes 1966080 | tf_op jit(solution)/shard_map/dot_general | solution.py:27
  47.9 1.5 fusion.34
  49.4 1.4 copy.81
  50.8 35.6 %all_to_all.26 = bf16[3,1024,256]{2,0,1:T(4,128)(2,1)S(1)} all-to-all(bf16[3,1024,256]{2,0,1:T(4,128)(2,1)S(1)} %copy.81), channel_id=1, replica_groups=mesh['section'=4,'trial'=128] {'section'}, dimensions={1} | all-to-all | bytes 3145728 | tf_op jit(solution)/shard_map/all_to_all | solution.py:55
  88.0 1.8 %convolution_bitcast_fusion.1 = f32[256,2,256]{2,0,1:T(8,128)S(1)} fusion(bf16[1024,2,256]{2,0,1:T(8,128)(2,1)} %all-gather.5.cloned.1.call-done, bf16[256,1024,1]{0,1,2:T(8,128)(2,1)S(1)} %bitcast.77), kind=kOutput, calls=%fused_computation.17 | convolution fusion | flops 268435456 | bytes 2097152 | tf_op jit(solution)/shard_map/dot_general | solution.py:27
  90.7 2.6 %fusion.4 = bf16[128,2,4,256]{0,3,2,1:T(8,128)(2,1)} fusion(f32[256,2,256]{2,0,1:T(8,128)} %get-tuple-element.158, bf16[1024,2,256]{2,0,1:T(8,128)(2,1)S(1)} %copy-done.1, bf16[256,1024,1]{0,1,2:T(8,128)(2,1)S(1)} %bitcast.78, bf16[128,4,2,256]{3,2,1,0:T(2,128)(2,1)S(1)} %bitcast.71, f32[256,2,192]{2,0,1:T(8,128)S(1)} %slice.61, f32[256,2,224]{2,0,1:T(8,128)S(1)} %slice.59), kind=kOutput, calls=%fused_computation.15 | convolution fusion | flops 403439616 | bytes 3997696 | tf_op jit(solution)/shard_map/jbil,cil->jibc/dot_general | solution.py:75
  93.3 2.2 %copy.96 = bf16[128,2,4,256]{3,2,1,0:T(4,128)(2,1)} copy(bf16[128,2,4,256]{0,3,2,1:T(8,128)(2,1)} %fusion.4) | data formatting | bytes 1048576 | tf_op jit(solution)/shard_map/convert_element_type | solution.py:79
  95.5 19.6 %all-to-all-start.2 = ((bf16[128,2,4,256]{3,2,1,0:T(4,128)(2,1)}), bf16[128,2,4,256]{3,2,1,0:T(4,128)(2,1)S(1)}, u32[]{:S(2)}, u32[]{:S(2)}) async-start(bf16[128,2,4,256]{3,2,1,0:T(4,128)(2,1)} %copy.96), calls=%async_computation.2 | async-start | bytes 1048576 | tf_op jit(solution)/shard_map/all_to_all | solution.py:78
  115.1 1.3 dynamic-slice
  117.4 37.0 %all-reduce.4 = s32[256]{0:T(256)S(1)} all-reduce(s32[256]{0:T(256)S(1)} %dynamic-update-slice), channel_id=1, replica_groups=mesh['section'=4,'trial'=128] {'trial'}, use_global_device_ids=true, to_apply=%add.4 | all-reduce | flops 256 | bytes 2048
  154.6 13.8 %while.14 = (s32[]{:T(128)}, f32[128,1024]{1,0:T(8,128)S(1)}, s32[128]{0:T(128)S(1)}, s32[256]{0:T(256)S(1)}, f32[256,1024]{1,0:T(8,128)S(1)}, /*index=5*/s32[]{:T(128)}, s32[]{:T(128)}) while((s32[]{:T(128)}, f32[128,1024]{1,0:T(8,128)S(1)}, s32[128]{0:T(128)S(1)}, s32[256]{0:T(256)S(1)}, f32[256,1024]{1,0:T(8,128)S(1)}, ...), condition=%wide.region_2.3_spmd.clone, body=%wide.region_1.2_spmd.clone.sunk | while | flops 527491 | bytes 2630751 | solution.py:95
  154.7 1.3 gather_fusion.1
  156.0 0.8 gather_fusion
  157.0 1.3 gather_fusion.1
  159.3 1.3 gather_fusion.1
  161.6 1.3 gather_fusion.1
  163.9 1.3 gather_fusion.1
  166.2 1.3 gather_fusion.1
  167.5 0.8 gather_fusion
  168.5 0.9 convert_element_type.61
  (71 shorter events, 10.3 us)
Async XLA Ops:
  6.5 84.1 %copy-start = (bf16[512,2,256]{2,1,0:T(2,128)(2,1)S(1)}, bf16[512,2,256]{2,1,0:T(2,128)(2,1)}, u32[]{:S(2)}) copy-start(bf16[512,2,256]{2,1,0:T(2,128)(2,1)} %param.9) | copy-start | bytes 1572868
  6.5 39.2 %all-gather.3.cloned.1.call-start = ((), (), s32[]{:S(2)}) async-start(), calls=%async_computation.3 | async-start | bytes 1310720 | tf_op jit(solution)/shard_map/all_gather | solution.py:41
  8.6 79.4 %all-gather.5.cloned.1.call-start = ((), (), s32[]{:S(2)}) async-start(), calls=%async_computation.4 | async-start | bytes 1310720 | tf_op jit(solution)/shard_map/all_gather | solution.py:41
  37.6 10.2 %copy-start.3 = (bf16[256,2,256]{2,1,0:T(2,128)(2,1)S(1)}, bf16[256,2,256]{2,1,0:T(2,128)(2,1)}, u32[]{:S(2)}) copy-start(bf16[256,2,256]{2,1,0:T(2,128)(2,1)} %param.12) | copy-start | bytes 786436
  37.6 10.2 %copy-start.5 = (bf16[256,2,256]{2,1,0:T(2,128)(2,1)S(1)}, bf16[256,2,256]{2,1,0:T(2,128)(2,1)}, u32[]{:S(2)}) copy-start(bf16[256,2,256]{2,1,0:T(2,128)(2,1)} %param.10) | copy-start | bytes 786436
  45.7 1.9 %copy-start.4 = (bf16[1024,2,256]{2,0,1:T(8,128)(2,1)S(1)}, bf16[1024,2,256]{2,0,1:T(8,128)(2,1)}, u32[]{:S(2)}) copy-start(bf16[1024,2,256]{2,0,1:T(8,128)(2,1)} %all-gather.3.cloned.1.call-done) | copy-start | bytes 3145732
  47.9 1.5 copy-start.2
  88.0 2.0 %copy-start.1 = (bf16[1024,2,256]{2,0,1:T(8,128)(2,1)S(1)}, bf16[1024,2,256]{2,0,1:T(8,128)(2,1)}, u32[]{:S(2)}) copy-start(bf16[1024,2,256]{2,0,1:T(8,128)(2,1)} %all-gather.5.cloned.1.call-done) | copy-start | bytes 3145732
  93.3 23.8 %copy-start.6 = (s32[2]{0:T(128)S(1)}, s32[2]{0:T(128)}, u32[]{:S(2)}) copy-start(s32[2]{0:T(128)} %param.15) | copy-start | bytes 28
  95.5 59.0 %all-to-all-start.2 = ((bf16[128,2,4,256]{3,2,1,0:T(4,128)(2,1)}), bf16[128,2,4,256]{3,2,1,0:T(4,128)(2,1)S(1)}, u32[]{:S(2)}, u32[]{:S(2)}) async-start(bf16[128,2,4,256]{3,2,1,0:T(4,128)(2,1)} %copy.96), calls=%async_computation.2 | async-start | bytes 1048576 | tf_op jit(solution)/shard_map/all_to_all | solution.py:78
Sparse Core Ops, SparseCore 0:
  9.5 36.1 all-gather.2
  49.5 38.4 all-gather.4
